TPU v7x, 32 devices: a whole 2x2x4 slice. The times are simulated.
32 devices in a mesh: seq: 8 (over y, x, core), head: 4 (over z).
Axes of the slice: x: 2, y: 2, z: 4, core: 2. Of those that a mesh axis runs over, the one named last changes fastest.
Arguments:
- query: bfloat16 [4096, 4096], P('seq', 'head'), may hold values from -6 to 6
- keys: bfloat16 [4096, 4096], P('seq', 'head'), may hold values from -6 to 6
- values: bfloat16 [4096, 4096], P('seq', 'head'), may hold values from -6 to 6
- log_decay: float32 [32, 4096], P('head', 'seq'), may hold values from -1 to 0, as said below
- beta: float32 [32, 4096], P('head', 'seq'), may hold values from 0.002 to 0.1
- level_weights: float32 [7, 32, 4096], P(None, 'head', 'seq'), may hold values from 0.25 to 4
- norm_gain: float32 [4096], P('head'), may hold values from 0.1 to 1.9
- out_weight: bfloat16 [4096, 4096], P('head'), may hold values from -0.09375 to 0.09375
Outputs:
- mixed: bfloat16 [4096, 4096], P(('seq', 'head'))
Inputs may be any that keep to these rules, and one draw needn't show every extreme that they name: log_decay is negative everywhere.
All inputs are finite; a program needn't handle non-finite values.
Results may differ from a plain program's by a relative error of at most 0.014.
Values may be sent and summed in bfloat16 or wider, within the bound.
A program may use at most 128 MiB of HBM per device.

v0:
```python
import functools

import jax
import jax.numpy as jnp
from jax import lax
from jax.experimental import pallas as pl
from jax.experimental.pallas import tpu as pltpu
from jax.sharding import PartitionSpec as P

BLK = 64
HALF = 256
MESH = pl.DeviceIdType.MESH
F32 = jnp.float32
B16 = jnp.bfloat16


def mm(left, right):
    return jnp.dot(left, right, preferred_element_type=F32)


def mm_t(left, right):
    return lax.dot_general(left, right, (((1,), (1,)), ((), ())), preferred_element_type=F32)


def mm_tl(left, right):
    return lax.dot_general(left, right, (((0,), (0,)), ((), ())), preferred_element_type=F32)


def unit_rows(matrix):
    return matrix * lax.rsqrt(jnp.sum(matrix * matrix, -1, keepdims=True) + 1e-06)


def places(rows, cols):
    return (
        lax.broadcasted_iota(jnp.int32, (rows, cols), 0),
        lax.broadcasted_iota(jnp.int32, (rows, cols), 1),
    )


def unit_lower_inverses(lowers):
    row, col = places(HALF, HALF)

    def same(size):
        return (row // size) == (col // size)

    eye = jnp.where(row == col, 1.0, 0.0)
    ys = [jnp.where(same(16), -low, 0.0) for low in lowers]
    yb = [y.astype(B16) for y in ys]
    y2 = [mm(y, y) for y in yb]
    y2b = [y.astype(B16) for y in y2]
    y3 = [mm(y, z) for y, z in zip(yb, y2b)]
    y4b = [mm(y, y).astype(B16) for y in y2b]
    first = [eye + a + b + c for a, b, c in zip(ys, y2, y3)]
    y8b = [mm(y, y).astype(B16) for y in y4b]
    second = [a + mm(a.astype(B16), y) for a, y in zip(first, y4b)]
    xs = [a + mm(a.astype(B16), y) for a, y in zip(second, y8b)]
    size = 16
    while size < HALF:
        ring = same(2 * size) & jnp.logical_not(same(size))
        xb = [x.astype(B16) for x in xs]
        inner = [
            mm(jnp.where(ring, low, 0.0).astype(B16), x).astype(B16) for low, x in zip(lowers, xb)
        ]
        xs = [x - mm(b, t) for x, b, t in zip(xs, xb, inner)]
        size *= 2
    return [x.astype(B16) for x in xs]


def attention_kernel(
    heads, rounds, depth,
    q_ref, k_ref, v_ref, decay_ref, beta_ref, weight_ref, gain_ref,
    o_ref,
    running, rows, local, seen, own, carry, cross, send, recv, send_sem, recv_sem,
):
    step = pl.program_id(0)
    me = lax.axis_index("seq")
    tokens = q_ref.shape[0]
    width = q_ref.shape[1]

    def partner(r):
        bit = (me // (1 << r)) % 2
        return me + (1 - 2 * bit) * (1 << r), bit

    def copy(r, head):
        return pltpu.make_async_remote_copy(
            src_ref=send.at[r, head],
            dst_ref=recv.at[r, head],
            send_sem=send_sem.at[r, head],
            recv_sem=recv_sem.at[r, head],
            device_id={"seq": partner(r)[0]},
            device_id_type=MESH,
        )

    @pl.when(step == 0)
    def _():
        barrier = pltpu.get_barrier_semaphore()
        for r in range(rounds):
            pl.semaphore_signal(
                barrier, inc=1, device_id={"seq": partner(r)[0]}, device_id_type=MESH
            )
        pl.semaphore_wait(barrier, rounds)
        total = decay_ref[...]
        lane = lax.broadcasted_iota(jnp.int32, total.shape, 1)
        shift = 1
        while shift < tokens:
            total = total + jnp.where(lane >= shift, pltpu.roll(total, shift, 1), 0.0)
            shift *= 2
        running[...] = total
        rows[...] = jnp.zeros_like(rows)

    @pl.when(step < heads)
    def _():
        head = step
        rows[0:1, :] = running[pl.ds(head, 1), :]
        rows[1:2, :] = beta_ref[pl.ds(head, 1), :]
        for level in range(1 + depth):
            rows[2 + level : 3 + level, :] = weight_ref[level, pl.ds(head, 1), :]
        run_row = rows[0:1, :]
        cols = rows[...].T
        run = cols[:, 0:1]
        beta = cols[:, 1:2]
        gamma = jnp.exp(run)
        end = run[tokens - 1 : tokens, :]
        qn = unit_rows(q_ref[...].astype(F32))
        kn = unit_rows(k_ref[...].astype(F32))
        qb = qn.astype(B16)
        kb = kn.astype(B16)
        fresh = (beta * v_ref[...].astype(F32)).astype(B16)
        faded = (beta * gamma * kn).astype(B16)
        pair = jnp.concatenate([fresh, faded], -1)
        tail = (jnp.exp(end - run) * kn).astype(B16)
        row, col = places(HALF, HALF)
        lo, hi = slice(0, HALF), slice(HALF, 2 * HALF)

        def decay(i, j):
            gap = jnp.exp(jnp.minimum(run[i] - run_row[:, j], 0.0))
            return jnp.where(row >= col, gap, 0.0) if i == j else gap

        d00, d10, d11 = decay(lo, lo), decay(hi, lo), decay(hi, hi)
        below = row > col
        l00 = jnp.where(below, beta[lo] * d00 * mm_t(kb[lo], kb[lo]), 0.0)
        l11 = jnp.where(below, beta[hi] * d11 * mm_t(kb[hi], kb[hi]), 0.0)
        l10 = (beta[hi] * d10 * mm_t(kb[hi], kb[lo])).astype(B16)
        m00 = (d00 * mm_t(qb[lo], kb[lo])).astype(B16)
        m11 = (d11 * mm_t(qb[hi], kb[hi])).astype(B16)
        m10 = (d10 * mm_t(qb[hi], kb[lo])).astype(B16)
        x00, x11 = unit_lower_inverses([l00, l11])
        x10 = (-mm(x11, mm(l10, x00).astype(B16))).astype(B16)
        p00 = mm(m00, x00)
        p11 = mm(m11, x11)
        p10 = (mm(m10, x00) + mm(m11, x10)).astype(B16)

        def level_weight(i):
            chosen = cols[i, 1 + depth : 2 + depth]
            for level in range(depth - 2, -1, -1):
                span = BLK << level
                chosen = jnp.where(
                    (row // span) == (col // span), cols[i, 2 + level : 3 + level], chosen
                )
            return chosen

        both = mm(p10, pair[lo])
        local[head, lo, :] = mm((level_weight(lo) * p00).astype(B16), fresh[lo])
        local[head, hi, :] = (
            mm((level_weight(hi) * p11).astype(B16), fresh[hi])
            + cols[hi, 2 + depth : 3 + depth] * both[:, :width]
        )
        seen[head, lo, :] = (gamma[lo] * qn[lo] - mm(p00.astype(B16), faded[lo])).astype(B16)
        seen[head, hi, :] = (
            gamma[hi] * qn[hi] - both[:, width:] - mm(p11.astype(B16), faded[hi])
        ).astype(B16)
        r0 = (mm_tl(tail[lo], x00) + mm_tl(tail[hi], x10)).astype(B16)
        r1 = mm_tl(tail[hi], x11).astype(B16)
        states = mm(r0, pair[lo]) + mm(r1, pair[hi])
        a, b = places(width, width)
        transit = jnp.where(a == b, jnp.exp(end), 0.0) - states[:, width:]
        own[head, 0] = transit
        own[head, 1] = states[:, :width]
        send[0, head, 0] = transit.astype(B16)
        send[0, head, 1] = states[:, :width].astype(B16)
        copy(0, head).start()

    for r in range(rounds):
        head = step - 1 - r

        @pl.when((head >= 0) & (head < heads))
        def _():
            copy(r, head).wait_recv()
            upper = partner(r)[1] == 1
            got_t, got_e = recv[r, head, 0], recv[r, head, 1]
            if r == 0:
                a, b = places(width, width)
                far_state = got_e.astype(F32)
                moved = got_t.astype(F32)
                kept = jnp.where(a == b, 1.0, 0.0)
            else:
                kept = carry[head]
                both = mm(kept.astype(B16), jnp.concatenate([got_t, got_e], -1))
                moved, far_state = both[:, :width], both[:, width:]
            cross[head, :, r * width : (r + 1) * width] = jnp.where(
                upper, far_state, 0.0
            ).astype(B16)
            if r < rounds - 1:
                carry[head] = jnp.where(upper, moved, kept)
                mine_t, mine_e = own[head, 0], own[head, 1]
                left = jnp.where(upper, mine_t, got_t.astype(F32)).astype(B16)
                right_t = jnp.where(upper, got_t.astype(F32), mine_t).astype(B16)
                right_e = jnp.where(upper, got_e.astype(F32), mine_e).astype(B16)
                later = jnp.where(upper, mine_e, got_e.astype(F32))
                joined = mm(left, jnp.concatenate([right_t, right_e], -1))
                new_t = joined[:, :width]
                new_e = joined[:, width:] + later
                own[head, 0] = new_t
                own[head, 1] = new_e
                send[r + 1, head, 0] = new_t.astype(B16)
                send[r + 1, head, 1] = new_e.astype(B16)
                copy(r + 1, head).start()

    @pl.when(step >= rounds)
    def _():
        head = step - rounds
        for r in range(rounds):
            rows[2 + r : 3 + r, :] = weight_ref[1 + depth + r, pl.ds(head, 1), :]
        cols = rows[...].T
        far = mm(seen[head], cross[head])
        total = local[head]
        for r in range(rounds):
            total = total + cols[:, 2 + r : 3 + r] * far[:, r * width : (r + 1) * width]
        scaled = total * lax.rsqrt(jnp.mean(total * total, -1, keepdims=True) + 1e-06)
        o_ref[...] = (scaled * gain_ref[...]).astype(B16)

        for r in range(rounds):
            copy(r, head).wait_send()


def attention(query, keys, values, log_decay, beta, level_weights, norm_gain):
    tokens = query.shape[0]
    heads = log_decay.shape[0]
    width = query.shape[1] // heads
    levels = level_weights.shape[0]
    rounds = lax.axis_size("seq").bit_length() - 1
    depth = levels - 1 - rounds

    def head_in(i):
        return (0, jnp.minimum(i, heads - 1))

    def head_out(i):
        return (0, jnp.maximum(i - rounds, 0))

    token_block = pl.BlockSpec((tokens, width), head_in)
    whole2 = pl.BlockSpec((heads, tokens), lambda i: (0, 0))
    return pl.pallas_call(
        functools.partial(attention_kernel, heads, rounds, depth),
        grid=(heads + rounds,),
        out_shape=jax.ShapeDtypeStruct((tokens, heads * width), B16),
        in_specs=[
            token_block, token_block, token_block, whole2, whole2,
            pl.BlockSpec((levels, heads, tokens), lambda i: (0, 0, 0)),
            pl.BlockSpec((1, width), head_out),
        ],
        out_specs=pl.BlockSpec((tokens, width), head_out),
        scratch_shapes=[
            pltpu.VMEM((heads, tokens), F32),
            pltpu.VMEM((16, tokens), F32),
            pltpu.VMEM((heads, tokens, width), F32),
            pltpu.VMEM((heads, tokens, width), B16),
            pltpu.VMEM((heads, 2, width, width), F32),
            pltpu.VMEM((heads, width, width), F32),
            pltpu.VMEM((heads, width, rounds * width), B16),
            pltpu.VMEM((rounds, heads, 2, width, width), B16),
            pltpu.VMEM((rounds, heads, 2, width, width), B16),
            pltpu.SemaphoreType.DMA((rounds, heads)),
            pltpu.SemaphoreType.DMA((rounds, heads)),
        ],
        compiler_params=pltpu.CompilerParams(
            collective_id=0, has_side_effects=True, vmem_limit_bytes=48 << 20
        ),
    )(query, keys, values, log_decay, beta, level_weights, norm_gain.reshape(1, -1))


def per_device(query, keys, values, log_decay, beta, level_weights, norm_gain, out_weight):
    normed = attention(query, keys, values, log_decay, beta, level_weights, norm_gain)
    return lax.psum_scatter(
        jnp.dot(normed, out_weight, preferred_element_type=F32).astype(B16),
        "head",
        scatter_dimension=0,
        tiled=True,
    )


def solution(mesh):
    placed = (
        P("seq", "head"),
        P("seq", "head"),
        P("seq", "head"),
        P("head", "seq"),
        P("head", "seq"),
        P(None, "head", "seq"),
        P("head"),
        P("head", None),
    )
    return jax.shard_map(
        per_device, mesh=mesh, in_specs=placed, out_specs=P(("seq", "head"), None), check_vma=False
    )
```

profile of v0, /device:TPU:0, one launch (start us, length us, event | category | flops | bytes accessed | tf_op | source)
XLA Modules:
  0.0 158.0 jit_solution(9991056142594371715)
XLA Ops:
  6.5 0.0 reduce-scatter.2.cloned.1.call-start
  6.5 0.0 copy-start
  6.5 1.2 copy-done
  7.8 0.0 copy-start.1
  7.8 1.2 copy-done.1
  9.0 0.0 copy-start.2
  9.0 1.2 copy-done.2
  10.2 0.0 copy-start.3
  10.2 0.9 copy-done.3
  11.1 0.0 copy-start.4
  11.1 0.7 copy-done.4
  11.8 0.0 copy-start.5
  11.8 0.7 copy-done.5
  12.5 0.0 copy-start.6
  12.6 0.7 copy-done.6
  13.2 51.3 %shard_map.82 = bf16[512,1024]{1,0:T(8,128)(2,1)S(1)} custom-call(bf16[512,1024]{1,0:T(8,128)(2,1)S(1)} %copy-done, bf16[512,1024]{1,0:T(8,128)(2,1)S(1)} %copy-done.1, bf16[512,1024]{1,0:T(8,128)(2,1)S(1)} %copy-done.2, f32[8,512]{1,0:T(8,128)S(1)} %copy-done.4, f32[8,512]{1,0:T(8,128)S(1)} %copy-done.5, f32[7,8,512]{2,1,0:T(8,128)S(1)} %copy-done.3, ...), custom_call_target="tpu_custom_call" | custom-call | tf_op jit(solution)/shard_map/pallas_call | solution.py:252
  64.5 9.4 %convolution_convert_fusion = bf16[512,4096]{1,0:T(8,128)(2,1)} fusion(bf16[512,1024]{1,0:T(8,128)(2,1)S(1)} %shard_map.82, bf16[1024,4096]{1,0:T(8,128)(2,1)} %param.15), kind=kOutput, calls=%fused_computation | convolution fusion | flops 4297064448 | bytes 13631488 | tf_op jit(solution)/shard_map/dot_general | solution.py:284
  73.9 0.0 reduce-scatter.2.cloned.1.call-update
  73.9 77.2 %reduce-scatter.2.cloned.1.call-done = bf16[128,4096]{1,0:T(8,128)(2,1)} async-done(((bf16[512,4096]{1,0:T(8,128)(2,1)}), bf16[128,4096]{1,0:T(8,128)(2,1)}) %reduce-scatter.2.cloned.1.call-update) | async-done | bytes 1048592 | tf_op jit(solution)/shard_map/reduce_scatter | solution.py:283
Async XLA Ops:
  6.5 144.6 %reduce-scatter.2.cloned.1.call-start = ((), (), s32[]{:S(2)}) async-start(), calls=%async_computation.1 | async-start | bytes 5242880 | tf_op jit(solution)/shard_map/reduce_scatter | solution.py:283
  6.5 1.2 copy-start
  7.8 1.2 copy-start.1
  9.0 1.2 copy-start.2
  10.2 0.9 copy-start.3
  11.1 0.7 copy-start.4
  11.8 0.7 copy-start.5
  12.5 0.7 copy-start.6
Sparse Core Ops, SparseCore 0:
  74.1 77.0 reduce-scatter.1
where the time goes:
time: 158 us
  waiting for transfers between devices  77.2 us (49%)
  Pallas kernels  51.3 us (32%)
  between operations  13.4 us (8%)
  matrix products  9.4 us (6%)
  local copies, waits for them, and re-layouts  6.69 us (4%)
    reduce_scatter x1, waiting for transfers between devices, per_device(): lax.psum_scatter(jnp.dot(normed, out_weight, preferred_element_type=F32)....  77.2 us
    pallas_call x1, Pallas kernels, attention(): pl.pallas_call(functools.partial(attention_kernel, heads, rounds, depth),...  51.3 us
    dot_general x1, matrix products, per_device(): jnp.dot(normed, out_weight, preferred_element_type=F32).astype(B16)  9.4 us
    unnamed x14, local copies, waits for them, and re-layouts  6.69 us
  transfers between devices with their start and end apart: 1, of which 1 were waited for; matrix products, arithmetic and copies ran while one was open for 0% of the time, Pallas kernels for 0%

commit v1 on v0

v1 whole, which is shorter than its diff:
```python
import functools

import jax
import jax.numpy as jnp
from jax import lax
from jax.experimental import pallas as pl
from jax.experimental.pallas import tpu as pltpu
from jax.sharding import PartitionSpec as P

BLK = 64
HALF = 256
MESH = pl.DeviceIdType.MESH
F32 = jnp.float32
B16 = jnp.bfloat16


def mm(left, right):
    return jnp.dot(left, right, preferred_element_type=F32)


def mm_t(left, right):
    return lax.dot_general(left, right, (((1,), (1,)), ((), ())), preferred_element_type=F32)


def mm_tl(left, right):
    return lax.dot_general(left, right, (((0,), (0,)), ((), ())), preferred_element_type=F32)


def unit_rows(matrix):
    return matrix * lax.rsqrt(jnp.sum(matrix * matrix, -1, keepdims=True) + 1e-06)


def places(rows, cols):
    return (
        lax.broadcasted_iota(jnp.int32, (rows, cols), 0),
        lax.broadcasted_iota(jnp.int32, (rows, cols), 1),
    )


def unit_lower_inverses(lowers):
    row, col = places(HALF, HALF)
    apart = row ^ col
    eye = jnp.where(row == col, 1.0, 0.0)
    ys = [jnp.where(apart < 16, -low, 0.0) for low in lowers]
    yb = [y.astype(B16) for y in ys]
    y2 = [mm(y, y) for y in yb]
    y2b = [y.astype(B16) for y in y2]
    y3 = [mm(y, z) for y, z in zip(yb, y2b)]
    y4b = [mm(y, y).astype(B16) for y in y2b]
    first = [eye + a + b + c for a, b, c in zip(ys, y2, y3)]
    y8b = [mm(y, y).astype(B16) for y in y4b]
    second = [a + mm(a.astype(B16), y) for a, y in zip(first, y4b)]
    xs = [a + mm(a.astype(B16), y) for a, y in zip(second, y8b)]
    size = 16
    while size < HALF:
        ring = (apart >= size) & (apart < 2 * size)
        xb = [x.astype(B16) for x in xs]
        inner = [
            mm(jnp.where(ring, low, 0.0).astype(B16), x).astype(B16) for low, x in zip(lowers, xb)
        ]
        xs = [x - mm(b, t) for x, b, t in zip(xs, xb, inner)]
        size *= 2
    return [x.astype(B16) for x in xs]


def attention_kernel(
    heads, group, rounds, depth,
    q_ref, k_ref, v_ref, decay_ref, beta_ref, weight_ref, gain_ref,
    o_ref,
    running, rows, local, seen, own, carry, cross, send, recv, send_sem, recv_sem,
):
    step = pl.program_id(0)
    me = lax.axis_index("seq")
    tokens = q_ref.shape[0]
    width = q_ref.shape[1] // group
    groups = heads // group

    def partner(r):
        bit = (me // (1 << r)) % 2
        return me + (1 - 2 * bit) * (1 << r), bit

    def copy(r, part):
        first = 1 if r == rounds - 1 else 0
        return pltpu.make_async_remote_copy(
            src_ref=send.at[r, part, pl.ds(first, 2 - first)],
            dst_ref=recv.at[r, part, pl.ds(first, 2 - first)],
            send_sem=send_sem.at[r, part],
            recv_sem=recv_sem.at[r, part],
            device_id={"seq": partner(r)[0]},
            device_id_type=MESH,
        )

    @pl.when(step == 0)
    def _():
        barrier = pltpu.get_barrier_semaphore()
        for r in range(rounds):
            pl.semaphore_signal(
                barrier, inc=1, device_id={"seq": partner(r)[0]}, device_id_type=MESH
            )
        pl.semaphore_wait(barrier, rounds)
        total = decay_ref[...]
        lane = lax.broadcasted_iota(jnp.int32, total.shape, 1)
        shift = 1
        while shift < tokens:
            total = total + jnp.where(lane >= shift, pltpu.roll(total, shift, 1), 0.0)
            shift *= 2
        running[...] = total
        rows[...] = jnp.zeros_like(rows)

    @pl.when(step < groups)
    def _():
        part = step
        row, col = places(HALF, HALF)
        apart = row ^ col
        on_below = row >= col
        below = row > col
        lo, hi = slice(0, HALF), slice(HALF, 2 * HALF)
        work = []
        for u in range(group):
            head = part * group + u
            rows[u, 0:1, :] = running[pl.ds(head, 1), :]
            rows[u, 1:2, :] = beta_ref[pl.ds(head, 1), :]
            for level in range(1 + depth):
                rows[u, 2 + level : 3 + level, :] = weight_ref[level, pl.ds(head, 1), :]
            run_row = rows[u, 0:1, :]
            cols = rows[u].T
            run = cols[:, 0:1]
            beta = cols[:, 1:2]
            gamma = jnp.exp(run)
            end = run[tokens - 1 : tokens, :]
            lanes = slice(u * width, (u + 1) * width)
            qn = unit_rows(q_ref[:, lanes].astype(F32))
            kn = unit_rows(k_ref[:, lanes].astype(F32))
            qb = qn.astype(B16)
            kb = kn.astype(B16)
            fresh = (beta * v_ref[:, lanes].astype(F32)).astype(B16)
            faded = (beta * gamma * kn).astype(B16)
            pair = jnp.concatenate([fresh, faded], -1)
            tail = (jnp.exp(end - run) * kn).astype(B16)

            def decay(i, j):
                gap = jnp.exp(jnp.minimum(run[i] - run_row[:, j], 0.0))
                return jnp.where(on_below, gap, 0.0) if i == j else gap

            d00, d10, d11 = decay(lo, lo), decay(hi, lo), decay(hi, hi)
            l00 = jnp.where(below, beta[lo] * d00 * mm_t(kb[lo], kb[lo]), 0.0)
            l11 = jnp.where(below, beta[hi] * d11 * mm_t(kb[hi], kb[hi]), 0.0)
            l10 = (beta[hi] * d10 * mm_t(kb[hi], kb[lo])).astype(B16)
            m00 = (d00 * mm_t(qb[lo], kb[lo])).astype(B16)
            m11 = (d11 * mm_t(qb[hi], kb[hi])).astype(B16)
            m10 = (d10 * mm_t(qb[hi], kb[lo])).astype(B16)
            work.append((cols, gamma, end, qn, fresh, faded, pair, tail, l00, l11, l10, m00, m11, m10))
        inverses = unit_lower_inverses([low for item in work for low in item[8:10]])
        x10s = [
            mm(item[10], inverses[2 * u]).astype(B16) for u, item in enumerate(work)
        ]
        x10s = [(-mm(inverses[2 * u + 1], x)).astype(B16) for u, x in enumerate(x10s)]
        for u, item in enumerate(work):
            head = part * group + u
            cols, gamma, end, qn, fresh, faded, pair, tail, _, _, _, m00, m11, m10 = item
            x00, x11, x10 = inverses[2 * u], inverses[2 * u + 1], x10s[u]
            p00 = mm(m00, x00)
            p11 = mm(m11, x11)
            p10 = (mm(m10, x00) + mm(m11, x10)).astype(B16)

            def level_weight(i):
                chosen = cols[i, 1 + depth : 2 + depth]
                for level in range(depth - 2, -1, -1):
                    chosen = jnp.where(apart < (BLK << level), cols[i, 2 + level : 3 + level], chosen)
                return chosen

            both = mm(p10, pair[lo])
            local[head, lo, :] = mm((level_weight(lo) * p00).astype(B16), fresh[lo])
            local[head, hi, :] = (
                mm((level_weight(hi) * p11).astype(B16), fresh[hi])
                + cols[hi, 2 + depth : 3 + depth] * both[:, :width]
            )
            seen[head, lo, :] = (gamma[lo] * qn[lo] - mm(p00.astype(B16), faded[lo])).astype(B16)
            seen[head, hi, :] = (
                gamma[hi] * qn[hi] - both[:, width:] - mm(p11.astype(B16), faded[hi])
            ).astype(B16)
            r0 = (mm_tl(tail[lo], x00) + mm_tl(tail[hi], x10)).astype(B16)
            r1 = mm_tl(tail[hi], x11).astype(B16)
            states = mm(r0, pair[lo]) + mm(r1, pair[hi])
            a, b = places(width, width)
            transit = jnp.where(a == b, jnp.exp(end), 0.0) - states[:, width:]
            own[head, 0] = transit
            own[head, 1] = states[:, :width]
            send[0, part, 0, u] = transit.astype(B16)
            send[0, part, 1, u] = states[:, :width].astype(B16)
        copy(0, part).start()

    for r in range(rounds):
        part = step - 1 - r

        @pl.when((part >= 0) & (part < groups))
        def _():
            copy(r, part).wait_recv()
            upper = partner(r)[1] == 1
            for u in range(group):
                head = part * group + u
                got_e = recv[r, part, 1, u]
                if r == rounds - 1:
                    kept = carry[head] if r > 0 else None
                    far_state = mm(kept.astype(B16), got_e) if r > 0 else got_e.astype(F32)
                    cross[head, :, r * width : (r + 1) * width] = jnp.where(
                        upper, far_state, 0.0
                    ).astype(B16)
                    continue
                got_t = recv[r, part, 0, u]
                if r == 0:
                    a, b = places(width, width)
                    far_state = got_e.astype(F32)
                    moved = got_t.astype(F32)
                    kept = jnp.where(a == b, 1.0, 0.0)
                else:
                    kept = carry[head]
                    both = mm(kept.astype(B16), jnp.concatenate([got_t, got_e], -1))
                    moved, far_state = both[:, :width], both[:, width:]
                cross[head, :, r * width : (r + 1) * width] = jnp.where(
                    upper, far_state, 0.0
                ).astype(B16)
                carry[head] = jnp.where(upper, moved, kept)
                mine_t, mine_e = own[head, 0], own[head, 1]
                left = jnp.where(upper, mine_t, got_t.astype(F32)).astype(B16)
                right_t = jnp.where(upper, got_t.astype(F32), mine_t).astype(B16)
                right_e = jnp.where(upper, got_e.astype(F32), mine_e).astype(B16)
                later = jnp.where(upper, mine_e, got_e.astype(F32))
                joined = mm(left, jnp.concatenate([right_t, right_e], -1))
                new_t = joined[:, :width]
                new_e = joined[:, width:] + later
                own[head, 0] = new_t
                own[head, 1] = new_e
                send[r + 1, part, 0, u] = new_t.astype(B16)
                send[r + 1, part, 1, u] = new_e.astype(B16)
            if r < rounds - 1:
                copy(r + 1, part).start()

    @pl.when(step >= rounds)
    def _():
        part = step - rounds
        for u in range(group):
            head = part * group + u
            lanes = slice(u * width, (u + 1) * width)
            for r in range(rounds):
                rows[u, 2 + r : 3 + r, :] = weight_ref[1 + depth + r, pl.ds(head, 1), :]
            cols = rows[u].T
            far = mm(seen[head], cross[head])
            total = local[head]
            for r in range(rounds):
                total = total + cols[:, 2 + r : 3 + r] * far[:, r * width : (r + 1) * width]
            scaled = total * lax.rsqrt(jnp.mean(total * total, -1, keepdims=True) + 1e-06)
            o_ref[:, lanes] = (scaled * gain_ref[:, lanes]).astype(B16)

        for r in range(rounds):
            copy(r, part).wait_send()


def attention(query, keys, values, log_decay, beta, level_weights, norm_gain):
    tokens = query.shape[0]
    heads = log_decay.shape[0]
    width = query.shape[1] // heads
    levels = level_weights.shape[0]
    rounds = lax.axis_size("seq").bit_length() - 1
    depth = levels - 1 - rounds
    group = 2
    groups = heads // group

    def head_in(i):
        return (0, jnp.minimum(i, groups - 1))

    def head_out(i):
        return (0, jnp.maximum(i - rounds, 0))

    token_block = pl.BlockSpec((tokens, group * width), head_in)
    whole2 = pl.BlockSpec((heads, tokens), lambda i: (0, 0))
    return pl.pallas_call(
        functools.partial(attention_kernel, heads, group, rounds, depth),
        grid=(groups + rounds,),
        out_shape=jax.ShapeDtypeStruct((tokens, heads * width), B16),
        in_specs=[
            token_block, token_block, token_block, whole2, whole2,
            pl.BlockSpec((levels, heads, tokens), lambda i: (0, 0, 0)),
            pl.BlockSpec((1, group * width), head_out),
        ],
        out_specs=pl.BlockSpec((tokens, group * width), head_out),
        scratch_shapes=[
            pltpu.VMEM((heads, tokens), F32),
            pltpu.VMEM((group, 16, tokens), F32),
            pltpu.VMEM((heads, tokens, width), F32),
            pltpu.VMEM((heads, tokens, width), B16),
            pltpu.VMEM((heads, 2, width, width), F32),
            pltpu.VMEM((heads, width, width), F32),
            pltpu.VMEM((heads, width, rounds * width), B16),
            pltpu.VMEM((rounds, groups, 2, group, width, width), B16),
            pltpu.VMEM((rounds, groups, 2, group, width, width), B16),
            pltpu.SemaphoreType.DMA((rounds, groups)),
            pltpu.SemaphoreType.DMA((rounds, groups)),
        ],
        compiler_params=pltpu.CompilerParams(
            collective_id=0, has_side_effects=True, vmem_limit_bytes=60 << 20
        ),
    )(query, keys, values, log_decay, beta, level_weights, norm_gain.reshape(1, -1))


def project_kernel(
    span, chunks, n_ref, w_ref, o_ref, parts, send, recv, send_sem, recv_sem
):
    step = pl.program_id(0)
    me = lax.axis_index("head")
    rows = o_ref.shape[0]
    has_left, has_right = me > 0, me < span - 1

    def rightward(dest, chunk):
        return pltpu.make_async_remote_copy(
            src_ref=send.at[dest, chunk],
            dst_ref=recv.at[dest, chunk],
            send_sem=send_sem.at[dest, chunk],
            recv_sem=recv_sem.at[dest, chunk],
            device_id={"head": me + 1},
            device_id_type=MESH,
        )

    def leftward(dest, chunk, slot):
        return pltpu.make_async_remote_copy(
            src_ref=send.at[dest, chunk],
            dst_ref=recv.at[slot, chunk],
            send_sem=send_sem.at[dest, chunk],
            recv_sem=recv_sem.at[slot, chunk],
            device_id={"head": me - 1},
            device_id_type=MESH,
        )

    def leftward_slot(dest):
        return jnp.where(dest == me - 1, span, dest)

    @pl.when(step == 0)
    def _():
        barrier = pltpu.get_barrier_semaphore()

        @pl.when(has_left)
        def _():
            pl.semaphore_signal(barrier, inc=1, device_id={"head": me - 1}, device_id_type=MESH)

        @pl.when(has_right)
        def _():
            pl.semaphore_signal(barrier, inc=1, device_id={"head": me + 1}, device_id_type=MESH)

        neighbours = jnp.where(has_left, 1, 0) + jnp.where(has_right, 1, 0)
        pl.semaphore_wait(barrier, neighbours)

    @pl.when(step < chunks)
    def _():
        chunk = step
        parts[chunk] = mm(n_ref[...], w_ref[...])

        for dest in range(span - 1, 0, -1):
            @pl.when(me == 0)
            def _():
                send[dest, chunk] = parts[chunk, dest * rows : (dest + 1) * rows, :].astype(B16)
                rightward(dest, chunk).start()

        for dest in range(span - 1):
            @pl.when(me == span - 1)
            def _():
                send[dest, chunk] = parts[chunk, dest * rows : (dest + 1) * rows, :].astype(B16)
                leftward(dest, chunk, leftward_slot(dest)).start()

    @pl.when(step >= chunks)
    def _():
        chunk = step - chunks

        for far in range(span - 1):
            right_dest, left_dest = span - 1 - far, far

            @pl.when(has_left & (right_dest > me))
            def _():
                rightward(right_dest, chunk).wait_recv()
                send[right_dest, chunk] = (
                    parts[chunk, right_dest * rows : (right_dest + 1) * rows, :]
                    + recv[right_dest, chunk].astype(F32)
                ).astype(B16)
                rightward(right_dest, chunk).start()

            @pl.when(has_right & (left_dest < me))
            def _():
                leftward(left_dest, chunk, left_dest).wait_recv()
                send[left_dest, chunk] = (
                    parts[chunk, left_dest * rows : (left_dest + 1) * rows, :]
                    + recv[left_dest, chunk].astype(F32)
                ).astype(B16)
                leftward(left_dest, chunk, leftward_slot(left_dest)).start()

        for dest in range(span):
            @pl.when(dest == me)
            def _():
                mine = parts[chunk, dest * rows : (dest + 1) * rows, :]
                if dest > 0:
                    rightward(dest, chunk).wait_recv()
                    mine = mine + recv[dest, chunk].astype(F32)
                if dest < span - 1:
                    leftward(dest, chunk, span).wait_recv()
                    mine = mine + recv[span, chunk].astype(F32)
                o_ref[...] = mine.astype(B16)

    @pl.when(step == 2 * chunks - 1)
    def _():
        @pl.loop(0, chunks)
        def _(chunk):
            for dest in range(span):
                @pl.when(dest > me)
                def _():
                    rightward(dest, chunk).wait_send()

                @pl.when(dest < me)
                def _():
                    leftward(dest, chunk, leftward_slot(dest)).wait_send()


def project(normed, out_weight):
    tokens, inner = normed.shape
    columns = out_weight.shape[1]
    span = lax.axis_size("head")
    rows = tokens // span
    piece = 512
    chunks = columns // piece
    return pl.pallas_call(
        functools.partial(project_kernel, span, chunks),
        grid=(2 * chunks,),
        out_shape=jax.ShapeDtypeStruct((rows, columns), B16),
        in_specs=[
            pl.BlockSpec((tokens, inner), lambda i: (0, 0)),
            pl.BlockSpec((inner, piece), lambda i: (0, jnp.minimum(i, chunks - 1))),
        ],
        out_specs=pl.BlockSpec((rows, piece), lambda i: (0, jnp.maximum(i - chunks, 0))),
        scratch_shapes=[
            pltpu.VMEM((chunks, tokens, piece), F32),
            pltpu.VMEM((span, chunks, rows, piece), B16),
            pltpu.VMEM((span + 1, chunks, rows, piece), B16),
            pltpu.SemaphoreType.DMA((span, chunks)),
            pltpu.SemaphoreType.DMA((span + 1, chunks)),
        ],
        compiler_params=pltpu.CompilerParams(
            collective_id=1, has_side_effects=True, vmem_limit_bytes=60 << 20
        ),
    )(normed, out_weight)


def per_device(query, keys, values, log_decay, beta, level_weights, norm_gain, out_weight):
    normed = attention(query, keys, values, log_decay, beta, level_weights, norm_gain)
    return project(normed, out_weight)


def solution(mesh):
    placed = (
        P("seq", "head"),
        P("seq", "head"),
        P("seq", "head"),
        P("head", "seq"),
        P("head", "seq"),
        P(None, "head", "seq"),
        P("head"),
        P("head", None),
    )
    return jax.shard_map(
        per_device, mesh=mesh, in_specs=placed, out_specs=P(("seq", "head"), None), check_vma=False
    )
```

time: 158 us -> 144 us (0.911)
  Pallas kernels: 51.3 us -> 141 us
  waiting for transfers between devices: 77.2 us -> 0 us
  between operations: 13.4 us -> 0.02 us
  matrix products: 9.4 us -> 0 us
  local copies, waits for them, and re-layouts: 6.69 us -> 2.29 us
    pallas_call x1 -> x2, Pallas kernels: 51.3 us -> 141 us  [the longest x1 101 us: project(): pl.pallas_call(functools.partial(project_kernel, span, chunks), grid=(2 *...]
    reduce_scatter x1 -> x0, waiting for transfers between devices: 77.2 us -> none  [per_device(): lax.psum_scatter(jnp.dot(normed, out_weight, preferred_element_type=F32)....]
    dot_general x1 -> x0, matrix products: 9.4 us -> none  [per_device(): jnp.dot(normed, out_weight, preferred_element_type=F32).astype(B16)]
    unnamed x14 -> x1, local copies, waits for them, and re-layouts: 6.69 us -> 2.29 us
  transfers between devices with their start and end apart: 1 -> 0, of which waited for: 1 -> 0; matrix products, arithmetic and copies ran while one was open for 0% -> 0% of each run, Pallas kernels for 0% -> 0%
where the time goes in v1:
time: 144 us; the launch traced here: 143 us
  Pallas kernels  141 us (98%)
  local copies, waits for them, and re-layouts  2.29 us (2%)
    pallas_call x1, Pallas kernels, project(): pl.pallas_call(functools.partial(project_kernel, span, chunks), grid=(2 *...  101 us
    pallas_call x1, Pallas kernels, attention(): pl.pallas_call(functools.partial(attention_kernel, heads, group, rounds,...  39.7 us

profile of v1, /device:TPU:0, one launch (start us, length us, event | category | flops | bytes accessed | tf_op | source)
XLA Modules:
  0.0 143.4 jit_solution(7964719064508353166)
XLA Ops:
  0.0 39.7 %shard_map.82.n_ref = bf16[512,1024]{1,0:T(8,128)(2,1)} custom-call(bf16[512,1024]{1,0:T(8,128)(2,1)} %q_ref.1, bf16[512,1024]{1,0:T(8,128)(2,1)} %k_ref.1, bf16[512,1024]{1,0:T(8,128)(2,1)} %v_ref.1, f32[8,512]{1,0:T(8,128)} %decay_ref.1, f32[8,512]{1,0:T(8,128)} %beta_ref.1, f32[7,8,512]{2,1,0:T(8,128)} %weight_ref.1, f32[1,1024]{1,0:T(1,128)} %bitcast.1), custom_call_target="tpu_custom_call" | custom-call | tf_op jit(solution)/shard_map/pallas_call | solution.py:277
  39.7 101.4 %shard_map.83 = bf16[128,4096]{1,0:T(8,128)(2,1)} custom-call(bf16[512,1024]{1,0:T(8,128)(2,1)} %shard_map.82.n_ref, bf16[1024,4096]{1,0:T(8,128)(2,1)} %w_ref.1), custom_call_target="tpu_custom_call" | custom-call | tf_op jit(solution)/shard_map/pallas_call | solution.py:427
  141.1 2.3 %copy.10 = bf16[128,4096]{1,0:T(8,128)(2,1)} copy(bf16[128,4096]{1,0:T(8,128)(2,1)} %shard_map.83) | data formatting | bytes 2097152

commit v2 on v1

--- a/solution.py
+++ b/solution.py
@@ -303,152 +303,17 @@
     )(query, keys, values, log_decay, beta, level_weights, norm_gain.reshape(1, -1))
 
 
-def project_kernel(
-    span, chunks, n_ref, w_ref, o_ref, parts, send, recv, send_sem, recv_sem
-):
-    step = pl.program_id(0)
-    me = lax.axis_index("head")
-    rows = o_ref.shape[0]
-    has_left, has_right = me > 0, me < span - 1
-
-    def rightward(dest, chunk):
-        return pltpu.make_async_remote_copy(
-            src_ref=send.at[dest, chunk],
-            dst_ref=recv.at[dest, chunk],
-            send_sem=send_sem.at[dest, chunk],
-            recv_sem=recv_sem.at[dest, chunk],
-            device_id={"head": me + 1},
-            device_id_type=MESH,
-        )
-
-    def leftward(dest, chunk, slot):
-        return pltpu.make_async_remote_copy(
-            src_ref=send.at[dest, chunk],
-            dst_ref=recv.at[slot, chunk],
-            send_sem=send_sem.at[dest, chunk],
-            recv_sem=recv_sem.at[slot, chunk],
-            device_id={"head": me - 1},
-            device_id_type=MESH,
-        )
-
-    def leftward_slot(dest):
-        return jnp.where(dest == me - 1, span, dest)
-
-    @pl.when(step == 0)
-    def _():
-        barrier = pltpu.get_barrier_semaphore()
-
-        @pl.when(has_left)
-        def _():
-            pl.semaphore_signal(barrier, inc=1, device_id={"head": me - 1}, device_id_type=MESH)
-
-        @pl.when(has_right)
-        def _():
-            pl.semaphore_signal(barrier, inc=1, device_id={"head": me + 1}, device_id_type=MESH)
-
-        neighbours = jnp.where(has_left, 1, 0) + jnp.where(has_right, 1, 0)
-        pl.semaphore_wait(barrier, neighbours)
-
-    @pl.when(step < chunks)
-    def _():
-        chunk = step
-        parts[chunk] = mm(n_ref[...], w_ref[...])
-
-        for dest in range(span - 1, 0, -1):
-            @pl.when(me == 0)
-            def _():
-                send[dest, chunk] = parts[chunk, dest * rows : (dest + 1) * rows, :].astype(B16)
-                rightward(dest, chunk).start()
-
-        for dest in range(span - 1):
-            @pl.when(me == span - 1)
-            def _():
-                send[dest, chunk] = parts[chunk, dest * rows : (dest + 1) * rows, :].astype(B16)
-                leftward(dest, chunk, leftward_slot(dest)).start()
-
-    @pl.when(step >= chunks)
-    def _():
-        chunk = step - chunks
-
-        for far in range(span - 1):
-            right_dest, left_dest = span - 1 - far, far
-
-            @pl.when(has_left & (right_dest > me))
-            def _():
-                rightward(right_dest, chunk).wait_recv()
-                send[right_dest, chunk] = (
-                    parts[chunk, right_dest * rows : (right_dest + 1) * rows, :]
-                    + recv[right_dest, chunk].astype(F32)
-                ).astype(B16)
-                rightward(right_dest, chunk).start()
-
-            @pl.when(has_right & (left_dest < me))
-            def _():
-                leftward(left_dest, chunk, left_dest).wait_recv()
-                send[left_dest, chunk] = (
-                    parts[chunk, left_dest * rows : (left_dest + 1) * rows, :]
-                    + recv[left_dest, chunk].astype(F32)
-                ).astype(B16)
-                leftward(left_dest, chunk, leftward_slot(left_dest)).start()
-
-        for dest in range(span):
-            @pl.when(dest == me)
-            def _():
-                mine = parts[chunk, dest * rows : (dest + 1) * rows, :]
-                if dest > 0:
-                    rightward(dest, chunk).wait_recv()
-                    mine = mine + recv[dest, chunk].astype(F32)
-                if dest < span - 1:
-                    leftward(dest, chunk, span).wait_recv()
-                    mine = mine + recv[span, chunk].astype(F32)
-                o_ref[...] = mine.astype(B16)
-
-    @pl.when(step == 2 * chunks - 1)
-    def _():
-        @pl.loop(0, chunks)
-        def _(chunk):
-            for dest in range(span):
-                @pl.when(dest > me)
-                def _():
-                    rightward(dest, chunk).wait_send()
-
-                @pl.when(dest < me)
-                def _():
-                    leftward(dest, chunk, leftward_slot(dest)).wait_send()
-
-
-def project(normed, out_weight):
-    tokens, inner = normed.shape
-    columns = out_weight.shape[1]
-    span = lax.axis_size("head")
-    rows = tokens // span
-    piece = 512
-    chunks = columns // piece
-    return pl.pallas_call(
-        functools.partial(project_kernel, span, chunks),
-        grid=(2 * chunks,),
-        out_shape=jax.ShapeDtypeStruct((rows, columns), B16),
-        in_specs=[
-            pl.BlockSpec((tokens, inner), lambda i: (0, 0)),
-            pl.BlockSpec((inner, piece), lambda i: (0, jnp.minimum(i, chunks - 1))),
-        ],
-        out_specs=pl.BlockSpec((rows, piece), lambda i: (0, jnp.maximum(i - chunks, 0))),
-        scratch_shapes=[
-            pltpu.VMEM((chunks, tokens, piece), F32),
-            pltpu.VMEM((span, chunks, rows, piece), B16),
-            pltpu.VMEM((span + 1, chunks, rows, piece), B16),
-            pltpu.SemaphoreType.DMA((span, chunks)),
-            pltpu.SemaphoreType.DMA((span + 1, chunks)),
-        ],
-        compiler_params=pltpu.CompilerParams(
-            collective_id=1, has_side_effects=True, vmem_limit_bytes=60 << 20
-        ),
-    )(normed, out_weight)
+def project(normed, weight):
+    shares = jnp.dot(normed, weight, preferred_element_type=F32).astype(B16)
+    return lax.psum_scatter(shares, "head", scatter_dimension=0, tiled=True)
 
 
 def per_device(query, keys, values, log_decay, beta, level_weights, norm_gain, out_weight):
     normed = attention(query, keys, values, log_decay, beta, level_weights, norm_gain)
-    return project(normed, out_weight)
+    cut = out_weight.shape[1] // 4
+    return jnp.concatenate(
+        [project(normed, out_weight[:, :cut]), project(normed, out_weight[:, cut:])], -1
+    )
 
 
 def solution(mesh):

time: 144 us -> 149 us (1.035)
  Pallas kernels: 141 us -> 39.7 us
  waiting for transfers between devices: 0 us -> 81.1 us
  between operations: 0.02 us -> 13.4 us
  matrix products: 0 us -> 11.8 us
  local copies, waits for them, and re-layouts: 2.29 us -> 0.01 us
  other arithmetic: 0 us -> 2.24 us
    pallas_call x1 -> x0, Pallas kernels: 101 us -> none  [project(): pl.pallas_call(functools.partial(project_kernel, span, chunks), grid=(2 *...]
    reduce_scatter x0 -> x2, waiting for transfers between devices: none -> 81.1 us  [project(): return lax.psum_scatter(shares, 'head', scatter_dimension=0, tiled=True)]
    dot_general x0 -> x2, matrix products: none -> 11.8 us  [project(): shares = jnp.dot(normed, weight, preferred_element_type=F32).astype(B16)]
    unnamed x1 -> x2, local copies, waits for them, and re-layouts: 2.29 us -> 0.01 us
    concatenate x0 -> x1, other arithmetic: none -> 2.24 us  [per_device(): jnp.concatenate([project(normed, out_weight[:, :cut]), project(normed, ou...]
  transfers between devices with their start and end apart: 0 -> 2, of which waited for: 0 -> 2; matrix products, arithmetic and copies ran while one was open for 0% -> 5% of each run, Pallas kernels for 0% -> 0%
where the time goes in v2:
time: 149 us; the launch traced here: 148 us
  waiting for transfers between devices  81.1 us (54%)
  Pallas kernels  39.7 us (27%)
  between operations  13.4 us (9%)
  matrix products  11.8 us (8%)
  other arithmetic  2.24 us (2%)
    reduce_scatter x2, waiting for transfers between devices, project(): return lax.psum_scatter(shares, 'head', scatter_dimension=0, tiled=True)  81.1 us
    pallas_call x1, Pallas kernels, attention(): pl.pallas_call(functools.partial(attention_kernel, heads, group, rounds,...  39.7 us
    dot_general x2, matrix products, project(): shares = jnp.dot(normed, weight, preferred_element_type=F32).astype(B16)  11.8 us
  transfers between devices with their start and end apart: 2, of which 2 were waited for; matrix products, arithmetic and copies ran while one was open for 5% of the time, Pallas kernels for 0%

profile of v2, /device:TPU:0, one launch (start us, length us, event | category | flops | bytes accessed | tf_op | source)
XLA Modules:
  0.0 148.3 jit_solution(834975181144681601)
XLA Ops:
  6.5 0.0 reduce-scatter.3.cloned.1.call-start
  6.5 39.7 %shard_map.82 = bf16[512,1024]{1,0:T(8,128)(2,1)} custom-call(bf16[512,1024]{1,0:T(8,128)(2,1)} %q_ref.1, bf16[512,1024]{1,0:T(8,128)(2,1)} %k_ref.1, bf16[512,1024]{1,0:T(8,128)(2,1)} %v_ref.1, f32[8,512]{1,0:T(8,128)} %decay_ref.1, f32[8,512]{1,0:T(8,128)} %beta_ref.1, f32[7,8,512]{2,1,0:T(8,128)} %weight_ref.1, f32[1,1024]{1,0:T(1,128)} %bitcast.3), custom_call_target="tpu_custom_call" | custom-call | tf_op jit(solution)/shard_map/pallas_call | solution.py:277
  46.3 0.0 copy-start
  46.3 4.2 %fusion.7 = bf16[512,1024]{1,0:T(8,128)(2,1)} fusion(bf16[512,1024]{1,0:T(8,128)(2,1)} %shard_map.82, bf16[1024,4096]{1,0:T(8,128)(2,1)} %param.15), kind=kOutput, calls=%fused_computation.5 | convolution fusion | flops 1074266112 | bytes 4194304 | tf_op jit(solution)/shard_map/dot_general | solution.py:307
  50.5 0.0 reduce-scatter.3.cloned.1.call-update
  50.5 0.0 reduce-scatter.5.cloned.1.call-start
  50.6 0.0 copy-done
  50.6 7.6 %fusion.2 = bf16[512,3072]{1,0:T(8,128)(2,1)} fusion(bf16[512,1024]{1,0:T(8,128)(2,1)S(1)} %copy-done, bf16[1024,4096]{1,0:T(8,128)(2,1)} %param.15), kind=kOutput, calls=%fused_computation.2 | convolution fusion | flops 3222798336 | bytes 10485760 | tf_op jit(solution)/shard_map/dot_general | solution.py:307
  58.1 0.0 reduce-scatter.5.cloned.1.call-update
  58.2 19.7 %reduce-scatter.3.cloned.1.call-done = bf16[128,1024]{1,0:T(8,128)(2,1)} async-done(((bf16[512,1024]{1,0:T(8,128)(2,1)}), bf16[128,1024]{1,0:T(8,128)(2,1)}) %reduce-scatter.3.cloned.1.call-update) | async-done | bytes 262160 | tf_op jit(solution)/shard_map/reduce_scatter | solution.py:308
  77.9 61.4 %reduce-scatter.5.cloned.1.call-done = bf16[128,3072]{1,0:T(8,128)(2,1)} async-done(((bf16[512,3072]{1,0:T(8,128)(2,1)}), bf16[128,3072]{1,0:T(8,128)(2,1)}) %reduce-scatter.5.cloned.1.call-update) | async-done | bytes 786448 | tf_op jit(solution)/shard_map/reduce_scatter | solution.py:308
  139.2 2.2 %pad_maximum_fusion = bf16[128,4096]{1,0:T(8,128)(2,1)} fusion(bf16[128,3072]{1,0:T(8,128)(2,1)} %reduce-scatter.5.cloned.1.call-done, bf16[128,1024]{1,0:T(8,128)(2,1)} %reduce-scatter.3.cloned.1.call-done), kind=kLoop, calls=%fused_computation.6 | loop fusion | flops 2097152 | bytes 2097152 | tf_op jit(solution)/shard_map/concatenate | solution.py:314
Async XLA Ops:
  6.5 71.3 %reduce-scatter.3.cloned.1.call-start = ((), (), s32[]{:S(2)}) async-start(), calls=%async_computation.2 | async-start | bytes 1310720 | tf_op jit(solution)/shard_map/reduce_scatter | solution.py:308
  46.3 4.3 %copy-start = (bf16[512,1024]{1,0:T(8,128)(2,1)S(1)}, bf16[512,1024]{1,0:T(8,128)(2,1)}, u32[]{:S(2)}) copy-start(bf16[512,1024]{1,0:T(8,128)(2,1)} %shard_map.82) | copy-start | bytes 3145732
  50.5 88.7 %reduce-scatter.5.cloned.1.call-start = ((), (), s32[]{:S(2)}) async-start(), calls=%async_computation.3 | async-start | bytes 3932160 | tf_op jit(solution)/shard_map/reduce_scatter | solution.py:308
Sparse Core Ops, SparseCore 0:
  50.6 27.1 reduce-scatter.2
  80.3 58.9 reduce-scatter.4

commit v3 on v1

--- a/solution.py
+++ b/solution.py
@@ -358,12 +358,22 @@
             @pl.when(me == 0)
             def _():
                 send[dest, chunk] = parts[chunk, dest * rows : (dest + 1) * rows, :].astype(B16)
+
+                @pl.when(chunk > 0)
+                def _():
+                    rightward(dest, chunk - 1).wait_send()
+
                 rightward(dest, chunk).start()
 
         for dest in range(span - 1):
             @pl.when(me == span - 1)
             def _():
                 send[dest, chunk] = parts[chunk, dest * rows : (dest + 1) * rows, :].astype(B16)
+
+                @pl.when(chunk > 0)
+                def _():
+                    leftward(dest, chunk - 1, leftward_slot(dest)).wait_send()
+
                 leftward(dest, chunk, leftward_slot(dest)).start()
 
     @pl.when(step >= chunks)
@@ -408,11 +418,13 @@
         @pl.loop(0, chunks)
         def _(chunk):
             for dest in range(span):
-                @pl.when(dest > me)
+                left_over = (chunk == chunks - 1) | (has_left & has_right)
+
+                @pl.when((dest > me) & left_over)
                 def _():
                     rightward(dest, chunk).wait_send()
 
-                @pl.when(dest < me)
+                @pl.when((dest < me) & left_over)
                 def _():
                     leftward(dest, chunk, leftward_slot(dest)).wait_send()
 

time: 144 us -> 144 us (level)
  no operation moved by 1% of the time
where the time goes in v3:
time: 144 us; the launch traced here: 143 us
  Pallas kernels  141 us (98%)
  local copies, waits for them, and re-layouts  2.29 us (2%)
    pallas_call x1, Pallas kernels, project(): pl.pallas_call(functools.partial(project_kernel, span, chunks), grid=(2 *...  101 us
    pallas_call x1, Pallas kernels, attention(): pl.pallas_call(functools.partial(attention_kernel, heads, group, rounds,...  39.7 us

profile of v3, /device:TPU:0, one launch (start us, length us, event | category | flops | bytes accessed | tf_op | source)
XLA Modules:
  0.0 143.5 jit_solution(6547658301180526829)
XLA Ops:
  0.0 39.7 %shard_map.82.n_ref = bf16[512,1024]{1,0:T(8,128)(2,1)} custom-call(bf16[512,1024]{1,0:T(8,128)(2,1)} %q_ref.1, bf16[512,1024]{1,0:T(8,128)(2,1)} %k_ref.1, bf16[512,1024]{1,0:T(8,128)(2,1)} %v_ref.1, f32[8,512]{1,0:T(8,128)} %decay_ref.1, f32[8,512]{1,0:T(8,128)} %beta_ref.1, f32[7,8,512]{2,1,0:T(8,128)} %weight_ref.1, f32[1,1024]{1,0:T(1,128)} %bitcast.1), custom_call_target="tpu_custom_call" | custom-call | tf_op jit(solution)/shard_map/pallas_call | solution.py:277
  39.7 101.4 %shard_map.83 = bf16[128,4096]{1,0:T(8,128)(2,1)} custom-call(bf16[512,1024]{1,0:T(8,128)(2,1)} %shard_map.82.n_ref, bf16[1024,4096]{1,0:T(8,128)(2,1)} %w_ref.1), custom_call_target="tpu_custom_call" | custom-call | tf_op jit(solution)/shard_map/pallas_call | solution.py:439
  141.2 2.3 %copy.10 = bf16[128,4096]{1,0:T(8,128)(2,1)} copy(bf16[128,4096]{1,0:T(8,128)(2,1)} %shard_map.83) | data formatting | bytes 2097152

commit v4 on v3

--- a/solution.py
+++ b/solution.py
@@ -263,7 +263,7 @@
     levels = level_weights.shape[0]
     rounds = lax.axis_size("seq").bit_length() - 1
     depth = levels - 1 - rounds
-    group = 2
+    group = 4 if heads % 4 == 0 else 1
     groups = heads // group
 
     def head_in(i):

time: 144 us -> 148 us (1.028)
  Pallas kernels: 141 us -> 145 us
    pallas_call x1, Pallas kernels: 39.7 us -> 44.2 us  [attention(): pl.pallas_call(functools.partial(attention_kernel, heads, group, rounds,...]
where the time goes in v4:
time: 148 us; the launch traced here: 147 us
  Pallas kernels  145 us (98%)
  local copies, waits for them, and re-layouts  2.29 us (2%)
    pallas_call x1, Pallas kernels, project(): pl.pallas_call(functools.partial(project_kernel, span, chunks), grid=(2 *...  101 us
    pallas_call x1, Pallas kernels, attention(): pl.pallas_call(functools.partial(attention_kernel, heads, group, rounds,...  44.2 us

profile of v4, /device:TPU:0, one launch (start us, length us, event | category | flops | bytes accessed | tf_op | source)
XLA Modules:
  0.0 147.5 jit_solution(6460150502741779633)
XLA Ops:
  0.0 44.2 %shard_map.82.n_ref = bf16[512,1024]{1,0:T(8,128)(2,1)} custom-call(bf16[512,1024]{1,0:T(8,128)(2,1)} %q_ref.1, bf16[512,1024]{1,0:T(8,128)(2,1)} %k_ref.1, bf16[512,1024]{1,0:T(8,128)(2,1)} %v_ref.1, f32[8,512]{1,0:T(8,128)} %decay_ref.1, f32[8,512]{1,0:T(8,128)} %beta_ref.1, f32[7,8,512]{2,1,0:T(8,128)} %weight_ref.1, f32[1,1024]{1,0:T(1,128)} %bitcast.1), custom_call_target="tpu_custom_call" | custom-call | tf_op jit(solution)/shard_map/pallas_call | solution.py:277
  44.2 100.9 %shard_map.83 = bf16[128,4096]{1,0:T(8,128)(2,1)} custom-call(bf16[512,1024]{1,0:T(8,128)(2,1)} %shard_map.82.n_ref, bf16[1024,4096]{1,0:T(8,128)(2,1)} %w_ref.1), custom_call_target="tpu_custom_call" | custom-call | tf_op jit(solution)/shard_map/pallas_call | solution.py:439
  145.2 2.3 %copy.10 = bf16[128,4096]{1,0:T(8,128)(2,1)} copy(bf16[128,4096]{1,0:T(8,128)(2,1)} %shard_map.83) | data formatting | bytes 2097152

commit v5 on v3

--- a/solution.py
+++ b/solution.py
@@ -434,7 +434,7 @@
     columns = out_weight.shape[1]
     span = lax.axis_size("head")
     rows = tokens // span
-    piece = 512
+    piece = 256
     chunks = columns // piece
     return pl.pallas_call(
         functools.partial(project_kernel, span, chunks),

time: 144 us -> 187 us (1.30)
  Pallas kernels: 141 us -> 184 us
    pallas_call x1, Pallas kernels: 101 us -> 145 us  [project(): pl.pallas_call(functools.partial(project_kernel, span, chunks), grid=(2 *...]
where the time goes in v5:
time: 187 us
  Pallas kernels  184 us (98%)
  local copies, waits for them, and re-layouts  2.29 us (1%)
    pallas_call x1, Pallas kernels, project(): pl.pallas_call(functools.partial(project_kernel, span, chunks), grid=(2 *...  145 us
    pallas_call x1, Pallas kernels, attention(): pl.pallas_call(functools.partial(attention_kernel, heads, group, rounds,...  39.7 us

profile of v5, /device:TPU:0, one launch (start us, length us, event | category | flops | bytes accessed | tf_op | source)
XLA Modules:
  0.0 186.7 jit_solution(1568129409261398332)
XLA Ops:
  0.0 39.7 %shard_map.82.n_ref = bf16[512,1024]{1,0:T(8,128)(2,1)} custom-call(bf16[512,1024]{1,0:T(8,128)(2,1)} %q_ref.1, bf16[512,1024]{1,0:T(8,128)(2,1)} %k_ref.1, bf16[512,1024]{1,0:T(8,128)(2,1)} %v_ref.1, f32[8,512]{1,0:T(8,128)} %decay_ref.1, f32[8,512]{1,0:T(8,128)} %beta_ref.1, f32[7,8,512]{2,1,0:T(8,128)} %weight_ref.1, f32[1,1024]{1,0:T(1,128)} %bitcast.1), custom_call_target="tpu_custom_call" | custom-call | tf_op jit(solution)/shard_map/pallas_call | solution.py:277
  39.7 144.7 %shard_map.83 = bf16[128,4096]{1,0:T(8,128)(2,1)} custom-call(bf16[512,1024]{1,0:T(8,128)(2,1)} %shard_map.82.n_ref, bf16[1024,4096]{1,0:T(8,128)(2,1)} %w_ref.1), custom_call_target="tpu_custom_call" | custom-call | tf_op jit(solution)/shard_map/pallas_call | solution.py:439
  184.4 2.3 %copy.10 = bf16[128,4096]{1,0:T(8,128)(2,1)} copy(bf16[128,4096]{1,0:T(8,128)(2,1)} %shard_map.83) | data formatting | bytes 2097152
